TPU v7x, 512 devices: a whole 4x8x8 slice. The times are simulated.
512 devices in a mesh: sen: 32 (over y, z_hi), par: 16 (over x, z_lo, core).
Axes of the slice: x: 4, y: 8, z: 8 (z_hi: 4, z_lo: 2; z = z_hi * 2 + z_lo), core: 2. Of those that a mesh axis runs over, the one named last changes fastest.
Arguments:
- vectors: float32 [2, 256, 256], P(None, 'sen'), may hold values from -6 to 6
- observed: float32 [2, 256, 256], P(None, 'sen'), may hold values from -6 to 6
- operator: bfloat16 [2, 128, 256, 6144], P(None, None, 'sen', 'par'), may hold values from -0.15625 to 0.15625
- noise: float32 [256], P('sen'), may hold values from 0.3 to 3
- coefficient: float32 [16, 384], P('par'), may hold values from 0.05 to 0.24
- offsets: int32 [16, 384], P('par'), may hold values from -3 to 3
Outputs:
- residual: float32 [2, 256, 256], P(None, 'sen')
- applied: float32 [2, 256, 256], P(None, 'sen')
All inputs are finite; a program needn't handle non-finite values.
Results may differ from a plain program's by a relative error of at most 0.0018.
Values may be sent and summed in bfloat16 or wider, within the bound.
A program may use at most 64 MiB of HBM per device.

v0:
```python
import math
import jax
import jax.numpy as jnp
from jax import lax
from jax.sharding import PartitionSpec as P

SWEEPS = 4


def padded_2(cells, sides, width):
    for axis, dim in sides:
        count = lax.axis_size(axis)
        ends = count - 1
        head = lax.slice_in_dim(cells, 0, width, axis=dim)
        tail = lax.slice_in_dim(cells, cells.shape[dim] - width, cells.shape[dim], axis=dim)
        cells = jnp.concatenate(
            [
                lax.ppermute(tail, axis, [(i, (i + 1) % count) for i in range(ends)]),
                cells,
                lax.ppermute(head, axis, [((i + 1) % count, i) for i in range(ends)]),
            ],
            axis=dim,
        )
    return cells


def make_basis(length):
    half = length // 2
    times = jnp.arange(length, dtype=jnp.int32)[:, None]
    freqs = jnp.arange(half, dtype=jnp.int32)[None, :]
    phase = (2 * freqs + 1) * times % (2 * length)
    angle = phase.astype(jnp.float32) * (math.pi / length)
    scale = math.sqrt(2.0 / length)
    return jnp.concatenate([jnp.cos(angle), jnp.sin(angle)], axis=1) * scale


def sweep_once(field, padded, coefficient, offsets):
    width = field.shape[-1]
    upper = padded[..., :-2, :]
    lower = padded[..., 2:, :]
    lower_pad = jnp.pad(lower, ((0, 0), (0, 0), (0, 0), (0, 0), (3, 3)))
    linked = jnp.zeros_like(field)
    for shift in range(-3, 4):
        linked = linked + jnp.where(
            offsets == shift, lower_pad[..., 3 + shift : 3 + shift + width], 0.0
        )
    sides = jnp.pad(field, ((0, 0), (0, 0), (0, 0), (0, 0), (1, 1)))
    return field + coefficient * (sides[..., :-2] + sides[..., 2:] + upper + linked - 4.0 * field)


def smooth(field, coefficient, offsets, extend):
    for sweep in range(SWEEPS):
        field = sweep_once(field, extend(field), coefficient, offsets)
    return field


def forward_part(operator, piece):
    count = piece.shape[1]
    rows = piece.shape[2]
    flat = piece.reshape(2, count, rows, piece.shape[3] * piece.shape[4])
    real = jnp.einsum(
        "fsp,frp->frs", operator[0], flat[0], preferred_element_type=jnp.float32
    ) - jnp.einsum("fsp,frp->frs", operator[1], flat[1], preferred_element_type=jnp.float32)
    imag = jnp.einsum(
        "fsp,frp->frs", operator[0], flat[1], preferred_element_type=jnp.float32
    ) + jnp.einsum("fsp,frp->frs", operator[1], flat[0], preferred_element_type=jnp.float32)
    return jnp.stack([real, imag])


def extend_whole(field):
    return padded_2(field, (("par", 3),), 1)


def hessian(record, operator, noise, coefficient, offsets, basis):
    rows, sensors, length = record.shape
    half = length // 2
    grid_rows, width = coefficient.shape
    spectrum = jnp.dot(
        record.reshape(rows * sensors, length), basis, precision=lax.Precision.HIGHEST
    )
    spectrum = spectrum.reshape(rows, sensors, 2, half).transpose(2, 3, 0, 1).astype(jnp.bfloat16)
    real = jnp.einsum(
        "frs,fsp->frp", spectrum[0], operator[0], preferred_element_type=jnp.float32
    ) + jnp.einsum("frs,fsp->frp", spectrum[1], operator[1], preferred_element_type=jnp.float32)
    imag = jnp.einsum(
        "frs,fsp->frp", spectrum[1], operator[0], preferred_element_type=jnp.float32
    ) - jnp.einsum("frs,fsp->frp", spectrum[0], operator[1], preferred_element_type=jnp.float32)
    partial_value = jnp.stack([real, imag]).reshape(2, half, rows, grid_rows, width)
    adjoint = lax.psum(partial_value, "sen")
    smoothed = smooth(adjoint, coefficient, offsets, extend_whole)
    prior = smoothed.astype(jnp.bfloat16)
    forward = forward_part(operator, prior)
    forward = lax.psum(forward, "par")
    forward = forward.transpose(2, 3, 0, 1).reshape(rows * sensors, length)
    back = jnp.dot(forward, basis.T, precision=lax.Precision.HIGHEST).reshape(rows, sensors, length)
    return back + noise[None, :, None] * record


def body(vectors, observed, operator, noise, coefficient, offsets):
    basis = make_basis(vectors.shape[-1])
    residual = observed - hessian(vectors, operator, noise, coefficient, offsets, basis)
    applied = hessian(residual, operator, noise, coefficient, offsets, basis)
    return (residual, applied)


def solution(mesh):
    placed = (
        P(None, "sen", None),
        P(None, "sen", None),
        P(None, None, "sen", "par"),
        P("sen"),
        P("par", None),
        P("par", None),
    )
    return jax.shard_map(
        body,
        mesh=mesh,
        in_specs=placed,
        out_specs=(P(None, "sen", None), P(None, "sen", None)),
        check_vma=False,
    )
```

profile of v0, /device:TPU:32, one launch (start us, length us, event | category | flops | bytes accessed | tf_op | source)
XLA Modules:
  0.0 1003.8 jit_solution(16166331370840971243)
XLA Ops:
  13.1 324.0 %all-reduce.19.cloned.1.call-done = f32[2,128,2,1,384]{4,2,1,0,3:T(2,128)} async-done(((f32[2,128,2,1,384]{4,2,1,0,3:T(2,128)}), f32[2,128,2,1,384]{4,2,1,0,3:T(2,128)}) %all-reduce.19.cloned.1.call-update) | async-done | bytes 786448 | tf_op jit(solution)/shard_map/psum | solution.py:89
  340.5 3.3 collective-permute-done.1
  343.8 8.0 multiply_add_fusion.5
  351.8 18.0 %collective-permute-start.2 = (f32[2,128,2,1,384]{4,2,1,0,3:T(2,128)S(1)}, f32[2,128,2,1,384]{4,2,1,0,3:T(2,128)S(1)}, u32[]{:S(2)}, u32[]{:S(2)}) collective-permute-start(f32[2,128,2,1,384]{4,2,1,0,3:T(2,128)S(1)} %multiply_add_fusion.5), channel_id=1, source_target_pairs={{0,1},{1,2},{2,3},{3,4},{4,5},{5,6},{6,7},{7,8},{8,9},{9,10},{10,1... | collective-permute-start | bytes 2359304 | tf_op jit(solution)/shard_map/ppermute | solution.py:18
  371.6 2.3 collective-permute-done.3
  374.0 6.8 multiply_add_fusion.4
  380.8 16.4 %collective-permute-start.4 = (f32[2,128,2,1,384]{4,2,1,0,3:T(2,128)S(1)}, f32[2,128,2,1,384]{4,2,1,0,3:T(2,128)S(1)}, u32[]{:S(2)}, u32[]{:S(2)}) collective-permute-start(f32[2,128,2,1,384]{4,2,1,0,3:T(2,128)S(1)} %multiply_add_fusion.4), channel_id=1, source_target_pairs={{0,1},{1,2},{2,3},{3,4},{4,5},{5,6},{6,7},{7,8},{8,9},{9,10},{10,1... | collective-permute-start | bytes 2359304 | tf_op jit(solution)/shard_map/ppermute | solution.py:18
  401.4 6.8 multiply_add_fusion.3
  408.2 17.8 %collective-permute-start.6 = (f32[2,128,2,1,384]{4,2,1,0,3:T(2,128)S(1)}, f32[2,128,2,1,384]{4,2,1,0,3:T(2,128)}, u32[]{:S(2)}, u32[]{:S(2)}) collective-permute-start(f32[2,128,2,1,384]{4,2,1,0,3:T(2,128)S(1)} %multiply_add_fusion.3), channel_id=1, source_target_pairs={{0,1},{1,2},{2,3},{3,4},{4,5},{5,6},{6,7},{7,8},{8,9},{9,10},{10,1... | collective-permute-start | bytes 2359304 | tf_op jit(solution)/shard_map/ppermute | solution.py:18
  427.7 2.7 collective-permute-done.7
  430.3 9.9 add_convert_fusion.1
  442.4 66.4 %psum.29 = f32[2,8,256]{2,1,0:T(8,128)S(1)} all-reduce(f32[2,8,256]{2,1,0:T(8,128)S(1)} %copy_bitcast_fusion.1), channel_id=1, replica_groups=mesh['sen'=32,'par'=16] {'par'}, use_global_device_ids=true, to_apply=%region_1.2 | all-reduce | flops 4096 | bytes 32768 | tf_op jit(solution)/shard_map/psum | solution.py:93
  512.7 314.5 %all-reduce.21.cloned.1.call-done = f32[2,128,2,1,384]{4,2,1,0,3:T(2,128)} async-done(((f32[2,128,2,1,384]{4,2,1,0,3:T(2,128)}), f32[2,128,2,1,384]{4,2,1,0,3:T(2,128)}) %all-reduce.21.cloned.1.call-update) | async-done | bytes 786448 | tf_op jit(solution)/shard_map/psum | solution.py:89
  830.6 3.3 collective-permute-done.9
  833.9 8.0 multiply_add_fusion.2
  841.9 18.0 %collective-permute-start.10 = (f32[2,128,2,1,384]{4,2,1,0,3:T(2,128)S(1)}, f32[2,128,2,1,384]{4,2,1,0,3:T(2,128)S(1)}, u32[]{:S(2)}, u32[]{:S(2)}) collective-permute-start(f32[2,128,2,1,384]{4,2,1,0,3:T(2,128)S(1)} %multiply_add_fusion.2), channel_id=1, source_target_pairs={{0,1},{1,2},{2,3},{3,4},{4,5},{5,6},{6,7},{7,8},{8,9},{9,10},{10,1... | collective-permute-start | bytes 2359304 | tf_op jit(solution)/shard_map/ppermute | solution.py:18
  864.1 6.8 multiply_add_fusion.1
  870.9 16.4 %collective-permute-start.12 = (f32[2,128,2,1,384]{4,2,1,0,3:T(2,128)S(1)}, f32[2,128,2,1,384]{4,2,1,0,3:T(2,128)S(1)}, u32[]{:S(2)}, u32[]{:S(2)}) collective-permute-start(f32[2,128,2,1,384]{4,2,1,0,3:T(2,128)S(1)} %multiply_add_fusion.1), channel_id=1, source_target_pairs={{0,1},{1,2},{2,3},{3,4},{4,5},{5,6},{6,7},{7,8},{8,9},{9,10},{10,1... | collective-permute-start | bytes 2359304 | tf_op jit(solution)/shard_map/ppermute | solution.py:18
  889.2 2.3 collective-permute-done.13
  891.5 6.8 multiply_add_fusion
  898.3 17.0 %collective-permute-start.14 = (f32[2,128,2,1,384]{4,2,1,0,3:T(2,128)S(1)}, f32[2,128,2,1,384]{4,2,1,0,3:T(2,128)S(1)}, u32[]{:S(2)}, u32[]{:S(2)}) collective-permute-start(f32[2,128,2,1,384]{4,2,1,0,3:T(2,128)S(1)} %multiply_add_fusion), channel_id=1, source_target_pairs={{0,1},{1,2},{2,3},{3,4},{4,5},{5,6},{6,7},{7,8},{8,9},{9,10},{10,1... | collective-permute-start | bytes 2359304 | tf_op jit(solution)/shard_map/ppermute | solution.py:18
  917.2 2.3 collective-permute-done.15
  919.5 6.8 add_convert_fusion
  928.5 67.5 %psum.31 = f32[2,8,256]{2,1,0:T(8,128)S(1)} all-reduce(f32[2,8,256]{2,1,0:T(8,128)S(1)} %copy_bitcast_fusion), channel_id=1, replica_groups=mesh['sen'=32,'par'=16] {'par'}, use_global_device_ids=true, to_apply=%region_3.4 | all-reduce | flops 4096 | bytes 32768 | tf_op jit(solution)/shard_map/psum | solution.py:93
  (76 shorter events, 37.3 us)
Async XLA Ops:
  7.2 329.9 %all-reduce.19.cloned.1.call-start = ((), (), s32[]{:S(2)}) async-start(), calls=%async_computation | async-start | bytes 1572864 | tf_op jit(solution)/shard_map/psum | solution.py:89
  11.8 328.0 %copy-start.5 = (f32[1,384]{1,0:T(1,128)S(1)}, f32[1,384]{1,0:T(1,128)}, u32[]{:S(2)}) copy-start(f32[1,384]{1,0:T(1,128)} %param.10) | copy-start | bytes 4612
  11.8 328.0 %copy-start.6 = (s32[1,384]{1,0:T(1,128)S(1)}, s32[1,384]{1,0:T(1,128)}, u32[]{:S(2)}) copy-start(s32[1,384]{1,0:T(1,128)} %param.11) | copy-start | bytes 4612
  13.1 814.2 %all-reduce.21.cloned.1.call-start = ((), (), s32[]{:S(2)}) async-start(), calls=%async_computation.1 | async-start | bytes 1572864 | tf_op jit(solution)/shard_map/psum | solution.py:89
  337.1 3.4 collective-permute-start
  338.4 5.3 collective-permute-start.1
  351.8 19.8 %collective-permute-start.2 = (f32[2,128,2,1,384]{4,2,1,0,3:T(2,128)S(1)}, f32[2,128,2,1,384]{4,2,1,0,3:T(2,128)S(1)}, u32[]{:S(2)}, u32[]{:S(2)}) collective-permute-start(f32[2,128,2,1,384]{4,2,1,0,3:T(2,128)S(1)} %multiply_add_fusion.5), channel_id=1, source_target_pairs={{0,1},{1,2},{2,3},{3,4},{4,5},{5,6},{6,7},{7,8},{8,9},{9,10},{10,1... | collective-permute-start | bytes 2359304 | tf_op jit(solution)/shard_map/ppermute | solution.py:18
  369.8 4.2 collective-permute-start.3
  380.8 18.3 %collective-permute-start.4 = (f32[2,128,2,1,384]{4,2,1,0,3:T(2,128)S(1)}, f32[2,128,2,1,384]{4,2,1,0,3:T(2,128)S(1)}, u32[]{:S(2)}, u32[]{:S(2)}) collective-permute-start(f32[2,128,2,1,384]{4,2,1,0,3:T(2,128)S(1)} %multiply_add_fusion.4), channel_id=1, source_target_pairs={{0,1},{1,2},{2,3},{3,4},{4,5},{5,6},{6,7},{7,8},{8,9},{9,10},{10,1... | collective-permute-start | bytes 2359304 | tf_op jit(solution)/shard_map/ppermute | solution.py:18
  397.2 4.2 collective-permute-start.5
  408.2 19.5 %collective-permute-start.6 = (f32[2,128,2,1,384]{4,2,1,0,3:T(2,128)S(1)}, f32[2,128,2,1,384]{4,2,1,0,3:T(2,128)}, u32[]{:S(2)}, u32[]{:S(2)}) collective-permute-start(f32[2,128,2,1,384]{4,2,1,0,3:T(2,128)S(1)} %multiply_add_fusion.3), channel_id=1, source_target_pairs={{0,1},{1,2},{2,3},{3,4},{4,5},{5,6},{6,7},{7,8},{8,9},{9,10},{10,1... | collective-permute-start | bytes 2359304 | tf_op jit(solution)/shard_map/ppermute | solution.py:18
  426.0 4.3 collective-permute-start.7
  441.8 67.0 %copy-start.2 = (f32[2,8,256]{2,1,0:T(8,128)S(1)}, f32[2,8,256]{2,1,0:T(8,128)}, u32[]{:S(2)}) copy-start(f32[2,8,256]{2,1,0:T(8,128)} %param.6) | copy-start | bytes 49156
  441.8 67.0 %copy-start.3 = (f32[2,8,256]{2,1,0:T(8,128)S(1)}, f32[2,8,256]{2,1,0:T(8,128)}, u32[]{:S(2)}) copy-start(f32[2,8,256]{2,1,0:T(8,128)} %param.7) | copy-start | bytes 49156
  441.9 66.9 %copy-start.4 = (f32[8]{0:T(128)S(1)}, f32[8]{0:T(128)}, u32[]{:S(2)}) copy-start(f32[8]{0:T(128)} %param.9) | copy-start | bytes 100
  509.1 486.9 %copy-start.1 = (f32[2,8,256]{2,1,0:T(8,128)}, f32[2,8,256]{2,1,0:T(8,128)S(1)}, u32[]{:S(2)}) copy-start(f32[2,8,256]{2,1,0:T(8,128)S(1)} %fusion.8) | copy-start | bytes 49156
  827.2 3.4 collective-permute-start.8
  828.6 5.3 collective-permute-start.9
  841.9 19.8 %collective-permute-start.10 = (f32[2,128,2,1,384]{4,2,1,0,3:T(2,128)S(1)}, f32[2,128,2,1,384]{4,2,1,0,3:T(2,128)S(1)}, u32[]{:S(2)}, u32[]{:S(2)}) collective-permute-start(f32[2,128,2,1,384]{4,2,1,0,3:T(2,128)S(1)} %multiply_add_fusion.2), channel_id=1, source_target_pairs={{0,1},{1,2},{2,3},{3,4},{4,5},{5,6},{6,7},{7,8},{8,9},{9,10},{10,1... | collective-permute-start | bytes 2359304 | tf_op jit(solution)/shard_map/ppermute | solution.py:18
  859.9 4.2 collective-permute-start.11
  870.9 18.3 %collective-permute-start.12 = (f32[2,128,2,1,384]{4,2,1,0,3:T(2,128)S(1)}, f32[2,128,2,1,384]{4,2,1,0,3:T(2,128)S(1)}, u32[]{:S(2)}, u32[]{:S(2)}) collective-permute-start(f32[2,128,2,1,384]{4,2,1,0,3:T(2,128)S(1)} %multiply_add_fusion.1), channel_id=1, source_target_pairs={{0,1},{1,2},{2,3},{3,4},{4,5},{5,6},{6,7},{7,8},{8,9},{9,10},{10,1... | collective-permute-start | bytes 2359304 | tf_op jit(solution)/shard_map/ppermute | solution.py:18
  887.3 4.2 collective-permute-start.13
  898.3 18.9 %collective-permute-start.14 = (f32[2,128,2,1,384]{4,2,1,0,3:T(2,128)S(1)}, f32[2,128,2,1,384]{4,2,1,0,3:T(2,128)S(1)}, u32[]{:S(2)}, u32[]{:S(2)}) collective-permute-start(f32[2,128,2,1,384]{4,2,1,0,3:T(2,128)S(1)} %multiply_add_fusion), channel_id=1, source_target_pairs={{0,1},{1,2},{2,3},{3,4},{4,5},{5,6},{6,7},{7,8},{8,9},{9,10},{10,1... | collective-permute-start | bytes 2359304 | tf_op jit(solution)/shard_map/ppermute | solution.py:18
  915.3 4.2 collective-permute-start.15
  (1 other events, 3.3 us)
Sparse Core Ops, SparseCore 0:
  13.2 323.8 all-reduce.18
  512.9 314.3 all-reduce.20
where the time goes:
time: 1000 us
  waiting for transfers between devices  663 us (66%)
  blocking collectives  134 us (13%)
  starting transfers between devices  117 us (12%)
  other arithmetic  63.2 us (6%)
  between operations  14.4 us (1%)
  matrix products  11.1 us (1%)
    psum x2, waiting for transfers between devices, hessian(): adjoint = lax.psum(partial_value, 'sen')  638 us
    psum x2, blocking collectives, hessian(): forward = lax.psum(forward, 'par')  134 us
    ppermute x8, starting transfers between devices, padded_2(): lax.ppermute(tail, axis, [(i, (i + 1) % count) for i in range(ends)])  106 us
    add x6, other arithmetic, sweep_once(): field + coefficient * (sides[..., :-2] + sides[..., 2:] + upper + linked...  43.3 us
    ppermute x8, waiting for transfers between devices, padded_2(): lax.ppermute(head, axis, [((i + 1) % count, i) for i in range(ends)])  20.8 us
  transfers between devices with their start and end apart: 18, of which 17 were waited for; matrix products, arithmetic and copies ran while one was open for 0% of the time, Pallas kernels for 0%

commit v1 on v0

--- a/solution.py
+++ b/solution.py
@@ -86,7 +86,7 @@
         "frs,fsp->frp", spectrum[1], operator[0], preferred_element_type=jnp.float32
     ) - jnp.einsum("frs,fsp->frp", spectrum[0], operator[1], preferred_element_type=jnp.float32)
     partial_value = jnp.stack([real, imag]).reshape(2, half, rows, grid_rows, width)
-    adjoint = lax.psum(partial_value, "sen")
+    adjoint = jnp.sum(lax.all_gather(partial_value, "sen"), axis=0)
     smoothed = smooth(adjoint, coefficient, offsets, extend_whole)
     prior = smoothed.astype(jnp.bfloat16)
     forward = forward_part(operator, prior)

time: 1000 us -> 984 us (0.984)
  the two profiles are of different devices: /device:TPU:32 before, /device:TPU:8 now
where the time goes in v1:
time: 984 us; the launch traced here: 983 us
  waiting for transfers between devices  621 us (63%)
  blocking collectives  134 us (14%)
  starting transfers between devices  118 us (12%)
  other arithmetic  79.9 us (8%)
  between operations  14.5 us (1%)
  matrix products  11.1 us (1%)
    all_gather x2, waiting for transfers between devices, hessian(): adjoint = jnp.sum(lax.all_gather(partial_value, 'sen'), axis=0)  589 us
    psum x2, blocking collectives, hessian(): forward = lax.psum(forward, 'par')  134 us
    ppermute x8, starting transfers between devices, padded_2(): lax.ppermute(tail, axis, [(i, (i + 1) % count) for i in range(ends)])  107 us
    add x6, other arithmetic, sweep_once(): field + coefficient * (sides[..., :-2] + sides[..., 2:] + upper + linked...  43.6 us
    ppermute x8, waiting for transfers between devices, padded_2(): lax.ppermute(head, axis, [((i + 1) % count, i) for i in range(ends)])  29.1 us
  transfers between devices with their start and end apart: 18, of which 17 were waited for; matrix products, arithmetic and copies ran while one was open for 0% of the time, Pallas kernels for 0%

profile of v1, /device:TPU:8, one launch (start us, length us, event | category | flops | bytes accessed | tf_op | source)
XLA Modules:
  0.0 983.4 jit_solution(6930456843251006270)
XLA Ops:
  13.2 299.9 %all-gather.5.cloned.1.call-done = f32[64,128,2,384]{3,1,2,0:T(8,128)} async-done(((f32[2,128,2,384]{3,1,2,0:T(8,128)}), f32[64,128,2,384]{3,1,2,0:T(8,128)}) %all-gather.5.cloned.1.call-update) | async-done | bytes 25165840 | tf_op jit(solution)/shard_map/all_gather | solution.py:89
  313.1 9.2 reduce.2
  326.1 7.4 collective-permute-done.1
  333.4 9.6 multiply_add_fusion.5
  343.0 18.4 %collective-permute-start.2 = (f32[2,128,2,1,384]{4,2,1,3,0:T(2,128)S(1)}, f32[2,128,2,1,384]{4,2,1,3,0:T(2,128)S(1)}, u32[]{:S(2)}, u32[]{:S(2)}) collective-permute-start(f32[2,128,2,1,384]{4,2,1,3,0:T(2,128)S(1)} %multiply_add_fusion.5), channel_id=1, source_target_pairs={{0,1},{1,2},{2,3},{3,4},{4,5},{5,6},{6,7},{7,8},{8,9},{9,10},{10,1... | collective-permute-start | bytes 2359304 | tf_op jit(solution)/shard_map/ppermute | solution.py:18
  363.3 2.3 collective-permute-done.3
  365.6 6.8 multiply_add_fusion.4
  372.4 16.8 %collective-permute-start.4 = (f32[2,128,2,1,384]{4,2,1,3,0:T(2,128)S(1)}, f32[2,128,2,1,384]{4,2,1,3,0:T(2,128)S(1)}, u32[]{:S(2)}, u32[]{:S(2)}) collective-permute-start(f32[2,128,2,1,384]{4,2,1,3,0:T(2,128)S(1)} %multiply_add_fusion.4), channel_id=1, source_target_pairs={{0,1},{1,2},{2,3},{3,4},{4,5},{5,6},{6,7},{7,8},{8,9},{9,10},{10,1... | collective-permute-start | bytes 2359304 | tf_op jit(solution)/shard_map/ppermute | solution.py:18
  393.4 6.8 multiply_add_fusion.3
  400.2 17.5 %collective-permute-start.6 = (f32[2,128,2,1,384]{4,2,1,3,0:T(2,128)S(1)}, f32[2,128,2,1,384]{4,2,1,3,0:T(2,128)}, u32[]{:S(2)}, u32[]{:S(2)}) collective-permute-start(f32[2,128,2,1,384]{4,2,1,3,0:T(2,128)S(1)} %multiply_add_fusion.3), channel_id=1, source_target_pairs={{0,1},{1,2},{2,3},{3,4},{4,5},{5,6},{6,7},{7,8},{8,9},{9,10},{10,1... | collective-permute-start | bytes 2359304 | tf_op jit(solution)/shard_map/ppermute | solution.py:18
  419.1 2.8 collective-permute-done.7
  421.9 9.9 %add_convert_fusion.1 = bf16[2,128,2,1,384]{4,2,1,3,0:T(2,128)(2,1)S(1)} fusion(f32[2,128,2,1,384]{4,2,1,3,0:T(2,128)S(1)} %multiply_add_fusion.3, f32[2,128,2,1,384]{4,2,1,3,0:T(2,128)} %collective-permute-done.6, f32[2,128,2,1,384]{4,2,1,3,0:T(2,128)} %collective-permute-done.7, pred[384]{0:T(512)(128)(4,1)S(1)} %get-tuple-element.7, ...), kind=kLoop, calls=%fused_computation.122 | loop fusion | flops 4128768 | bytes 2756736 | tf_op jit(solution)/shard_map/convert_element_type | solution.py:91
  434.1 66.6 %psum.14 = f32[2,8,256]{2,1,0:T(8,128)S(1)} all-reduce(f32[2,8,256]{2,1,0:T(8,128)S(1)} %copy_bitcast_fusion.3), channel_id=1, replica_groups=mesh['sen'=32,'par'=16] {'par'}, use_global_device_ids=true, to_apply=%region_1.2 | all-reduce | flops 4096 | bytes 32768 | tf_op jit(solution)/shard_map/psum | solution.py:93
  504.7 289.1 %all-gather.7.cloned.1.call-done = f32[64,128,2,384]{3,1,2,0:T(8,128)} async-done(((f32[2,128,2,384]{3,1,2,0:T(8,128)}), f32[64,128,2,384]{3,1,2,0:T(8,128)}) %all-gather.7.cloned.1.call-update) | async-done | bytes 25165840 | tf_op jit(solution)/shard_map/all_gather | solution.py:89
  793.7 9.2 reduce.3
  806.7 7.2 collective-permute-done.9
  813.9 6.8 multiply_add_fusion.2
  820.7 18.4 %collective-permute-start.10 = (f32[2,128,2,1,384]{4,2,1,3,0:T(2,128)S(1)}, f32[2,128,2,1,384]{4,2,1,3,0:T(2,128)S(1)}, u32[]{:S(2)}, u32[]{:S(2)}) collective-permute-start(f32[2,128,2,1,384]{4,2,1,3,0:T(2,128)S(1)} %multiply_add_fusion.2), channel_id=1, source_target_pairs={{0,1},{1,2},{2,3},{3,4},{4,5},{5,6},{6,7},{7,8},{8,9},{9,10},{10,1... | collective-permute-start | bytes 2359304 | tf_op jit(solution)/shard_map/ppermute | solution.py:18
  843.4 6.8 multiply_add_fusion.1
  850.2 16.9 %collective-permute-start.12 = (f32[2,128,2,1,384]{4,2,1,3,0:T(2,128)S(1)}, f32[2,128,2,1,384]{4,2,1,3,0:T(2,128)S(1)}, u32[]{:S(2)}, u32[]{:S(2)}) collective-permute-start(f32[2,128,2,1,384]{4,2,1,3,0:T(2,128)S(1)} %multiply_add_fusion.1), channel_id=1, source_target_pairs={{0,1},{1,2},{2,3},{3,4},{4,5},{5,6},{6,7},{7,8},{8,9},{9,10},{10,1... | collective-permute-start | bytes 2359304 | tf_op jit(solution)/shard_map/ppermute | solution.py:18
  871.2 6.8 multiply_add_fusion
  878.0 16.5 %collective-permute-start.14 = (f32[2,128,2,1,384]{4,2,1,3,0:T(2,128)S(1)}, f32[2,128,2,1,384]{4,2,1,3,0:T(2,128)S(1)}, u32[]{:S(2)}, u32[]{:S(2)}) collective-permute-start(f32[2,128,2,1,384]{4,2,1,3,0:T(2,128)S(1)} %multiply_add_fusion), channel_id=1, source_target_pairs={{0,1},{1,2},{2,3},{3,4},{4,5},{5,6},{6,7},{7,8},{8,9},{9,10},{10,1... | collective-permute-start | bytes 2359304 | tf_op jit(solution)/shard_map/ppermute | solution.py:18
  898.8 6.8 add_convert_fusion
  907.8 67.8 %psum.15 = f32[2,8,256]{2,1,0:T(8,128)S(1)} all-reduce(f32[2,8,256]{2,1,0:T(8,128)S(1)} %copy_bitcast_fusion.2), channel_id=1, replica_groups=mesh['sen'=32,'par'=16] {'par'}, use_global_device_ids=true, to_apply=%region_3.4 | all-reduce | flops 4096 | bytes 32768 | tf_op jit(solution)/shard_map/psum | solution.py:93
  (82 shorter events, 42.7 us)
Async XLA Ops:
  7.2 3.3 copy-start
  7.2 305.9 %all-gather.5.cloned.1.call-start = ((), (), s32[]{:S(2)}) async-start(), calls=%async_computation | async-start | bytes 25952256 | tf_op jit(solution)/shard_map/all_gather | solution.py:89
  13.1 780.6 %all-gather.7.cloned.1.call-start = ((), (), s32[]{:S(2)}) async-start(), calls=%async_computation.1 | async-start | bytes 25952256 | tf_op jit(solution)/shard_map/all_gather | solution.py:89
  322.2 3.3 copy-start.6
  322.9 3.2 collective-permute-start
  324.2 9.2 collective-permute-start.1
  343.0 20.3 %collective-permute-start.2 = (f32[2,128,2,1,384]{4,2,1,3,0:T(2,128)S(1)}, f32[2,128,2,1,384]{4,2,1,3,0:T(2,128)S(1)}, u32[]{:S(2)}, u32[]{:S(2)}) collective-permute-start(f32[2,128,2,1,384]{4,2,1,3,0:T(2,128)S(1)} %multiply_add_fusion.5), channel_id=1, source_target_pairs={{0,1},{1,2},{2,3},{3,4},{4,5},{5,6},{6,7},{7,8},{8,9},{9,10},{10,1... | collective-permute-start | bytes 2359304 | tf_op jit(solution)/shard_map/ppermute | solution.py:18
  361.4 4.2 collective-permute-start.3
  372.4 18.6 %collective-permute-start.4 = (f32[2,128,2,1,384]{4,2,1,3,0:T(2,128)S(1)}, f32[2,128,2,1,384]{4,2,1,3,0:T(2,128)S(1)}, u32[]{:S(2)}, u32[]{:S(2)}) collective-permute-start(f32[2,128,2,1,384]{4,2,1,3,0:T(2,128)S(1)} %multiply_add_fusion.4), channel_id=1, source_target_pairs={{0,1},{1,2},{2,3},{3,4},{4,5},{5,6},{6,7},{7,8},{8,9},{9,10},{10,1... | collective-permute-start | bytes 2359304 | tf_op jit(solution)/shard_map/ppermute | solution.py:18
  389.2 4.2 collective-permute-start.5
  400.2 18.9 %collective-permute-start.6 = (f32[2,128,2,1,384]{4,2,1,3,0:T(2,128)S(1)}, f32[2,128,2,1,384]{4,2,1,3,0:T(2,128)}, u32[]{:S(2)}, u32[]{:S(2)}) collective-permute-start(f32[2,128,2,1,384]{4,2,1,3,0:T(2,128)S(1)} %multiply_add_fusion.3), channel_id=1, source_target_pairs={{0,1},{1,2},{2,3},{3,4},{4,5},{5,6},{6,7},{7,8},{8,9},{9,10},{10,1... | collective-permute-start | bytes 2359304 | tf_op jit(solution)/shard_map/ppermute | solution.py:18
  417.6 4.3 collective-permute-start.7
  433.5 67.2 %copy-start.2 = (f32[2,8,256]{2,1,0:T(8,128)S(1)}, f32[2,8,256]{2,1,0:T(8,128)}, u32[]{:S(2)}) copy-start(f32[2,8,256]{2,1,0:T(8,128)} %param.6) | copy-start | bytes 49156
  433.5 67.2 %copy-start.3 = (f32[2,8,256]{2,1,0:T(8,128)S(1)}, f32[2,8,256]{2,1,0:T(8,128)}, u32[]{:S(2)}) copy-start(f32[2,8,256]{2,1,0:T(8,128)} %param.7) | copy-start | bytes 49156
  433.5 67.2 %copy-start.4 = (f32[8]{0:T(128)S(1)}, f32[8]{0:T(128)}, u32[]{:S(2)}) copy-start(f32[8]{0:T(128)} %param.9) | copy-start | bytes 100
  501.0 474.6 %copy-start.1 = (f32[2,8,256]{2,1,0:T(8,128)}, f32[2,8,256]{2,1,0:T(8,128)S(1)}, u32[]{:S(2)}) copy-start(f32[2,8,256]{2,1,0:T(8,128)S(1)} %fusion.8) | copy-start | bytes 49156
  803.5 3.2 collective-permute-start.8
  804.8 9.1 collective-permute-start.9
  820.7 20.3 %collective-permute-start.10 = (f32[2,128,2,1,384]{4,2,1,3,0:T(2,128)S(1)}, f32[2,128,2,1,384]{4,2,1,3,0:T(2,128)S(1)}, u32[]{:S(2)}, u32[]{:S(2)}) collective-permute-start(f32[2,128,2,1,384]{4,2,1,3,0:T(2,128)S(1)} %multiply_add_fusion.2), channel_id=1, source_target_pairs={{0,1},{1,2},{2,3},{3,4},{4,5},{5,6},{6,7},{7,8},{8,9},{9,10},{10,1... | collective-permute-start | bytes 2359304 | tf_op jit(solution)/shard_map/ppermute | solution.py:18
  839.2 4.2 collective-permute-start.11
  850.2 18.7 %collective-permute-start.12 = (f32[2,128,2,1,384]{4,2,1,3,0:T(2,128)S(1)}, f32[2,128,2,1,384]{4,2,1,3,0:T(2,128)S(1)}, u32[]{:S(2)}, u32[]{:S(2)}) collective-permute-start(f32[2,128,2,1,384]{4,2,1,3,0:T(2,128)S(1)} %multiply_add_fusion.1), channel_id=1, source_target_pairs={{0,1},{1,2},{2,3},{3,4},{4,5},{5,6},{6,7},{7,8},{8,9},{9,10},{10,1... | collective-permute-start | bytes 2359304 | tf_op jit(solution)/shard_map/ppermute | solution.py:18
  867.1 4.2 collective-permute-start.13
  878.0 18.4 %collective-permute-start.14 = (f32[2,128,2,1,384]{4,2,1,3,0:T(2,128)S(1)}, f32[2,128,2,1,384]{4,2,1,3,0:T(2,128)S(1)}, u32[]{:S(2)}, u32[]{:S(2)}) collective-permute-start(f32[2,128,2,1,384]{4,2,1,3,0:T(2,128)S(1)} %multiply_add_fusion), channel_id=1, source_target_pairs={{0,1},{1,2},{2,3},{3,4},{4,5},{5,6},{6,7},{7,8},{8,9},{9,10},{10,1... | collective-permute-start | bytes 2359304 | tf_op jit(solution)/shard_map/ppermute | solution.py:18
  894.6 4.2 collective-permute-start.15
  (1 other events, 3.3 us)
Sparse Core Ops, SparseCore 0:
  13.2 299.7 all-gather.4
  504.8 288.8 all-gather.6
